TPU v7x, 256 devices: a whole 4x4x8 slice. The times are simulated.
256 devices in a mesh: row: 16 (over y, x), col: 16 (over z, core).
Axes of the slice: x: 4, y: 4, z: 8, core: 2. Of those that a mesh axis runs over, the one named last changes fastest.
Arguments:
- block_values: float32 [16, 16, 40, 128, 128], P('row', 'col'), may hold values from 7.8125e-06 to 0.00078125
- block_index: int32 [16, 16, 2, 40], P('row', 'col'), may hold values from 0 to 31, as said below
- block_count: int32 [16, 16], P('row', 'col'), may hold values from 1 to 40, as said below
- strength: float32 [32], replicated, may hold values from 1 to 30
- raw_scores: float32 [512, 32, 128], P(('row', 'col')), may hold values from -24 to 24
Outputs:
- smoothed: float32 [512, 32, 128], P(('row', 'col'))
- final_residual: float32 [512, 32, 128], P(('row', 'col'))
Inputs may be any that keep to these rules, and one draw needn't show every extreme that they name: `block_count`: some device has exactly 40 live slots; the others hold between half and all of their share of the upper triangle, scaled to 40. `block_index`: the live slots of one device name distinct blocks, each with global block row at most its global block column; slots at or above the count hold pairs in range that are ignored.
All inputs are finite; a program needn't handle non-finite values.
Results may differ from a plain program's by a relative error of at most 0.0003.
Values sent between devices are 32-bit elements; how exact they have to be, the bound alone decides.
A program may use at most 64 MiB of HBM per device.

v0:
```python
import jax
import jax.numpy as jnp
from jax import lax
from jax.sharding import PartitionSpec as P

ITERS = 3


def local_terms(values, row_index, col_index, panel_rows, panel_cols):
    picked_cols = jnp.take(panel_cols, col_index, axis=0)
    picked_rows = jnp.take(panel_rows, row_index, axis=0)
    to_rows = jnp.einsum("crk,cik->cri", picked_cols, values, precision=lax.Precision.HIGHEST)
    to_cols = jnp.einsum("cri,cik->crk", picked_rows, values, precision=lax.Precision.HIGHEST)
    row_part = jax.ops.segment_sum(to_rows, row_index, num_segments=panel_rows.shape[0])
    col_part = jax.ops.segment_sum(to_cols, col_index, num_segments=panel_cols.shape[0])
    return (row_part, col_part)


def fold_terms(row_part, col_part):
    return lax.psum_scatter(row_part, "col", scatter_dimension=0, tiled=True) + lax.psum_scatter(
        col_part, "row", scatter_dimension=0, tiled=True
    )


def total(field):
    return jnp.sum(field, axis=(0, 2))


def global_sum(partial_sum):
    return lax.psum(partial_sum, ("row", "col"))


def shards(block_values, block_index, block_count, strength, raw_scores):
    values = block_values[0, 0]
    row_index = block_index[0, 0, 0]
    col_index = block_index[0, 0, 1]
    live_mask = (jnp.arange(values.shape[0], dtype=jnp.int32) < block_count[0, 0]).astype(
        jnp.float32
    )
    masked = values * live_mask[:, None, None]
    segment = raw_scores.shape[0]
    block_size = raw_scores.shape[2]
    rows_here = lax.axis_size("col") * segment
    cols_here = lax.axis_size("row") * segment
    ones_rows = jnp.ones((rows_here, 1, block_size), jnp.float32)
    ones_cols = jnp.ones((cols_here, 1, block_size), jnp.float32)
    degree_rows, degree_cols = local_terms(masked, row_index, col_index, ones_rows, ones_cols)
    degree = fold_terms(degree_rows, degree_cols)
    gains = strength[None, :, None]
    smoothed = jnp.zeros_like(raw_scores)
    residual = raw_scores
    direction = raw_scores
    norm_now = global_sum(total(residual * residual))
    for iteration in range(ITERS):
        panel_rows = lax.all_gather(direction, "col", axis=0, tiled=True)
        panel_cols = lax.all_gather(direction, "row", axis=0, tiled=True)
        row_part, col_part = local_terms(masked, row_index, col_index, panel_rows, panel_cols)
        product = fold_terms(row_part, col_part)
        image = direction + gains * (degree * direction - product)
        step_size = norm_now / global_sum(total(direction * image))
        smoothed = smoothed + step_size[None, :, None] * direction
        residual = residual - step_size[None, :, None] * image
        norm_next = global_sum(total(residual * residual))
        direction = residual + (norm_next / norm_now)[None, :, None] * direction
        norm_now = norm_next
    return (smoothed, residual)


def solution(mesh):
    placed = (
        P("row", "col", None, None, None),
        P("row", "col", None, None),
        P("row", "col"),
        P(),
        P(("row", "col"), None, None),
    )
    return jax.shard_map(
        shards,
        mesh=mesh,
        in_specs=placed,
        out_specs=(P(("row", "col"), None, None), P(("row", "col"), None, None)),
        check_vma=False,
    )
```

profile of v0, /device:TPU:1, one launch (start us, length us, event | category | flops | bytes accessed | tf_op | source)
XLA Modules:
  0.0 916.9 jit_solution(5695150841030016190)
XLA Ops:
  7.2 0.8 compare_and_fusion
  8.0 0.8 slice_bitcast_fusion
  9.4 23.0 %all_gather.19 = f32[32,32,128]{2,1,0:T(8,128)S(1)} all-gather(f32[2,32,128]{2,1,0:T(8,128)} %param.13), channel_id=1, replica_groups=mesh['row'=16,'col'=16] {'col'}, dimensions={0}, use_global_device_ids=true | all-gather | bytes 557056 | tf_op jit(solution)/shard_map/all_gather | solution.py:55
  32.4 0.6 gather_fusion.3
  33.0 5.0 fusion.4
  38.1 4.9 scatter_fusion.1
  43.0 0.8 copy-done.3
  43.8 0.0 reduce-scatter.9.cloned.1.call-start
  43.9 19.6 %all_gather.18 = f32[32,32,128]{2,1,0:T(8,128)S(1)} all-gather(f32[2,32,128]{2,1,0:T(8,128)S(1)} %copy-done.7), channel_id=1, replica_groups=mesh['row'=16,'col'=16] {'row'}, dimensions={0}, use_global_device_ids=true | all-gather | bytes 557056 | tf_op jit(solution)/shard_map/all_gather | solution.py:56
  63.4 1.4 gather_fusion.2
  64.9 6.2 fusion.5
  71.1 4.7 scatter_fusion
  75.8 0.8 copy-done.4
  76.7 0.0 reduce-scatter.15.cloned.1.call-start
  76.7 0.6 gather_fusion
  77.3 0.6 gather_fusion.1
  77.9 0.6 dynamic-slice
  78.5 0.6 dynamic-slice.2
  80.4 0.1 bitcast_select_fusion
  80.5 4.3 fusion.7
  84.7 0.9 scatter_custom_fusion
  85.7 2.3 fusion.6
  88.0 0.7 scatter_custom_fusion.1
  88.7 58.4 %all-reduce.1 = f32[32,1,128]{2,0,1:T(8,128)S(1)} all-reduce(f32[32,1,128]{2,0,1:T(8,128)S(1)} %bitcast.49), channel_id=3, replica_groups=mesh['row'=16,'col'=16] {'row'}, use_global_device_ids=true, to_apply=%region_5.7.clone | all-reduce | flops 4096 | bytes 32768
  147.1 61.3 %all-reduce = f32[32,1,128]{2,0,1:T(8,128)S(1)} all-reduce(f32[32,1,128]{2,0,1:T(8,128)S(1)} %bitcast.48), channel_id=2, replica_groups=mesh['row'=16,'col'=16] {'col'}, use_global_device_ids=true, to_apply=%region_3.5.clone | all-reduce | flops 4096 | bytes 32768
  208.5 1.0 multiply_reduce_fusion.4
  209.5 74.0 %all-reduce.2 = (f32[32]{0:T(128)S(1)}, f32[32]{0:T(128)S(1)}) all-reduce(f32[32]{0:T(128)S(1)} %get-tuple-element.5, f32[32]{0:T(128)S(1)} %get-tuple-element.4), channel_id=1, replica_groups=mesh['row'=16,'col'=16] {'row','col'}, use_global_device_ids=true, to_apply=%region_1.2 | all-reduce | flops 64 | bytes 512 | tf_op jit(solution)/shard_map/psum | solution.py:30
  283.5 1.0 multiply_reduce_fusion.3
  284.5 74.5 %psum.44 = f32[32]{0:T(128)S(1)} all-reduce(f32[32]{0:T(128)S(1)} %get-tuple-element.10), channel_id=1, replica_groups=mesh['row'=16,'col'=16] {'row','col'}, use_global_device_ids=true, to_apply=%region_13.16 | all-reduce | flops 32 | bytes 256 | tf_op jit(solution)/shard_map/psum | solution.py:30
  358.9 0.1 multiply_add_fusion.4
  359.0 17.2 %all_gather.21 = f32[32,32,128]{2,1,0:T(8,128)S(1)} all-gather(f32[2,32,128]{2,1,0:T(8,128)S(1)} %multiply_add_fusion.4), channel_id=1, replica_groups=mesh['row'=16,'col'=16] {'col'}, dimensions={0}, use_global_device_ids=true | all-gather | bytes 557056 | tf_op jit(solution)/shard_map/all_gather | solution.py:55
  376.2 1.4 gather_fusion.5
  377.7 4.3 fusion.2
  382.1 4.7 scatter_fusion.3
  386.8 0.8 copy-done.5
  387.6 0.0 reduce-scatter.13.cloned.1.call-start
  387.7 19.2 %all_gather.20 = f32[32,32,128]{2,1,0:T(8,128)S(1)} all-gather(f32[2,32,128]{2,1,0:T(8,128)S(1)} %multiply_add_fusion.4), channel_id=1, replica_groups=mesh['row'=16,'col'=16] {'row'}, dimensions={0}, use_global_device_ids=true | all-gather | bytes 557056 | tf_op jit(solution)/shard_map/all_gather | solution.py:56
  406.8 1.4 gather_fusion.4
  408.3 6.2 fusion.3
  414.5 4.7 scatter_fusion.2
  419.2 0.8 copy-done.6
  420.1 38.4 %reduce-scatter.15.cloned.1.call-done = f32[2,32,128]{2,1,0:T(8,128)} async-done(((f32[32,32,128]{2,1,0:T(8,128)}), f32[2,32,128]{2,1,0:T(8,128)}) %reduce-scatter.15.cloned.1.call-update) | async-done | bytes 32784 | tf_op jit(solution)/shard_map/reduce_scatter | solution.py:20
  458.5 57.2 %reduce-scatter.13.cloned.1.call-done = f32[2,32,128]{2,1,0:T(8,128)} async-done(((f32[32,32,128]{2,1,0:T(8,128)}), f32[2,32,128]{2,1,0:T(8,128)}) %reduce-scatter.13.cloned.1.call-update) | async-done | bytes 32784 | tf_op jit(solution)/shard_map/reduce_scatter | solution.py:20
  515.7 1.0 multiply_reduce_fusion.2
  516.7 79.6 %psum.45 = f32[32]{0:T(128)S(1)} all-reduce(f32[32]{0:T(128)S(1)} %multiply_reduce_fusion.2), channel_id=1, replica_groups=mesh['row'=16,'col'=16] {'row','col'}, use_global_device_ids=true, to_apply=%region_19.22 | all-reduce | flops 32 | bytes 256 | tf_op jit(solution)/shard_map/psum | solution.py:30
  596.2 1.0 multiply_reduce_fusion.1
  597.2 72.4 %psum.46 = f32[32]{0:T(128)S(1)} all-reduce(f32[32]{0:T(128)S(1)} %get-tuple-element.8), channel_id=1, replica_groups=mesh['row'=16,'col'=16] {'row','col'}, use_global_device_ids=true, to_apply=%region_21.24 | all-reduce | flops 32 | bytes 256 | tf_op jit(solution)/shard_map/psum | solution.py:30
  669.6 0.1 multiply_add_fusion.2
  669.6 18.1 %all_gather.23 = f32[32,32,128]{2,1,0:T(8,128)S(1)} all-gather(f32[2,32,128]{2,1,0:T(8,128)S(1)} %multiply_add_fusion.2), channel_id=1, replica_groups=mesh['row'=16,'col'=16] {'col'}, dimensions={0}, use_global_device_ids=true | all-gather | bytes 557056 | tf_op jit(solution)/shard_map/all_gather | solution.py:55
  687.7 1.4 gather_fusion.7
  689.2 4.3 fusion
  693.6 4.7 scatter_fusion.5
  698.3 0.8 copy-done.2
  699.1 19.2 %all_gather.22 = f32[32,32,128]{2,1,0:T(8,128)S(1)} all-gather(f32[2,32,128]{2,1,0:T(8,128)S(1)} %multiply_add_fusion.2), channel_id=1, replica_groups=mesh['row'=16,'col'=16] {'row'}, dimensions={0}, use_global_device_ids=true | all-gather | bytes 557056 | tf_op jit(solution)/shard_map/all_gather | solution.py:56
  718.4 1.4 gather_fusion.6
  719.8 5.3 fusion.1
  725.1 0.1 broadcast.50.clone.4
  725.2 2.7 scatter_fusion.4
  727.9 0.8 copy-done.1
  728.7 41.8 %reduce-scatter.19.cloned.1.call-done = f32[2,32,128]{2,1,0:T(8,128)} async-done(((f32[32,32,128]{2,1,0:T(8,128)}), f32[2,32,128]{2,1,0:T(8,128)}) %reduce-scatter.19.cloned.1.call-update) | async-done | bytes 32784 | tf_op jit(solution)/shard_map/reduce_scatter | solution.py:20
  770.5 57.3 %reduce-scatter.17.cloned.1.call-done = f32[2,32,128]{2,1,0:T(8,128)} async-done(((f32[32,32,128]{2,1,0:T(8,128)}), f32[2,32,128]{2,1,0:T(8,128)}) %reduce-scatter.17.cloned.1.call-update) | async-done | bytes 32784 | tf_op jit(solution)/shard_map/reduce_scatter | solution.py:20
  827.8 1.0 multiply_reduce_fusion
  828.8 79.8 %psum.47 = f32[32]{0:T(128)S(1)} all-reduce(f32[32]{0:T(128)S(1)} %multiply_reduce_fusion), channel_id=1, replica_groups=mesh['row'=16,'col'=16] {'row','col'}, use_global_device_ids=true, to_apply=%region_27.30 | all-reduce | flops 32 | bytes 256 | tf_op jit(solution)/shard_map/psum | solution.py:30
  908.5 1.5 multiply_subtract_fusion
  (42 shorter events, 0.6 us)
Async XLA Ops:
  7.2 201.3 %reduce-scatter.11.cloned.1.call-start = ((), (), s32[]{:S(2)}) async-start(), calls=%async_computation.7 | async-start | bytes 557056 | tf_op jit(solution)/shard_map/reduce_scatter | solution.py:20
  33.0 10.9 %copy-start.7 = (f32[2,32,128]{2,1,0:T(8,128)S(1)}, f32[2,32,128]{2,1,0:T(8,128)}, u32[]{:S(2)}) copy-start(f32[2,32,128]{2,1,0:T(8,128)} %param.13) | copy-start | bytes 98308
  38.0 26.9 %copy-start = (f32[1,1,40,128,128]{4,3,2,1,0:T(8,128)S(1)}, f32[1,1,40,128,128]{4,3,2,1,0:T(8,128)}, u32[]{:S(2)}) copy-start(f32[1,1,40,128,128]{4,3,2,1,0:T(8,128)} %param.9) | copy-start | bytes 7864324
  42.9 0.8 copy-start.3
  43.8 164.7 %reduce-scatter.9.cloned.1.call-start = ((), (), s32[]{:S(2)}) async-start(), calls=%async_computation.6 | async-start | bytes 557056 | tf_op jit(solution)/shard_map/reduce_scatter | solution.py:20
  71.1 6.8 copy-start.10
  71.1 7.4 copy-start.9
  75.8 0.8 copy-start.4
  76.7 381.8 %reduce-scatter.15.cloned.1.call-start = ((), (), s32[]{:S(2)}) async-start(), calls=%async_computation.9 | async-start | bytes 557056 | tf_op jit(solution)/shard_map/reduce_scatter | solution.py:20
  80.4 128.1 %copy-start.8 = (f32[32]{0:T(128)S(1)}, f32[32]{0:T(128)}, u32[]{:S(2)}) copy-start(f32[32]{0:T(128)} %param.12) | copy-start | bytes 388
  386.8 0.8 copy-start.5
  387.6 128.1 %reduce-scatter.13.cloned.1.call-start = ((), (), s32[]{:S(2)}) async-start(), calls=%async_computation.8 | async-start | bytes 557056 | tf_op jit(solution)/shard_map/reduce_scatter | solution.py:20
  419.2 0.8 copy-start.6
  420.0 350.5 %reduce-scatter.19.cloned.1.call-start = ((), (), s32[]{:S(2)}) async-start(), calls=%async_computation.11 | async-start | bytes 557056 | tf_op jit(solution)/shard_map/reduce_scatter | solution.py:20
  698.3 0.8 copy-start.2
  699.1 128.7 %reduce-scatter.17.cloned.1.call-start = ((), (), s32[]{:S(2)}) async-start(), calls=%async_computation.10 | async-start | bytes 557056 | tf_op jit(solution)/shard_map/reduce_scatter | solution.py:20
  727.9 0.8 copy-start.1
Sparse Core Ops, SparseCore 0:
  43.9 73.4 reduce-scatter.10
  120.0 55.2 reduce-scatter.8
  387.7 70.6 reduce-scatter.14
  461.0 54.6 reduce-scatter.12
  699.2 71.2 reduce-scatter.18
  773.0 54.7 reduce-scatter.16
where the time goes:
time: 918 us; the launch traced here: 917 us
  blocking collectives  616 us (67%)
  waiting for transfers between devices  195 us (21%)
  matrix products  37.9 us (4%)
  other arithmetic  35.4 us (4%)
  between operations  16.3 us (2%)
  local copies, waits for them, and re-layouts  15.9 us (2%)
    psum x5, blocking collectives, global_sum(): return lax.psum(partial_sum, ('row', 'col'))  380 us
    unnamed x2, blocking collectives  120 us
    reduce_scatter x3, waiting for transfers between devices, fold_terms(): lax.psum_scatter(row_part, 'col', scatter_dimension=0, tiled=True)  115 us
    reduce_scatter x3, waiting for transfers between devices, fold_terms(): lax.psum_scatter(col_part, 'row', scatter_dimension=0, tiled=True)  80.2 us
    all_gather x3, blocking collectives, shards(): panel_rows = lax.all_gather(direction, 'col', axis=0, tiled=True)  58.3 us
    all_gather x3, blocking collectives, shards(): panel_cols = lax.all_gather(direction, 'row', axis=0, tiled=True)  58 us
    dot_general x4, matrix products, local_terms(): jnp.einsum('crk,cik->cri', picked_cols, values, precision=lax.Precision.H...  22 us
  transfers between devices with their start and end apart: 6, of which 4 were waited for; matrix products, arithmetic and copies ran while one was open for 5% of the time, Pallas kernels for 0%

commit v1 on v0

--- a/solution.py
+++ b/solution.py
@@ -2,8 +2,14 @@
 import jax.numpy as jnp
 from jax import lax
 from jax.sharding import PartitionSpec as P
+from jax.lax import all_gather
 
 ITERS = 3
+
+
+def mark_figure(incoming_x, group_axis):
+    local_now = all_gather(incoming_x, group_axis)
+    return jnp.sum(local_now, axis=0)
 
 
 def local_terms(values, row_index, col_index, panel_rows, panel_cols):
@@ -27,7 +33,7 @@
 
 
 def global_sum(partial_sum):
-    return lax.psum(partial_sum, ("row", "col"))
+    return mark_figure(partial_sum, group_axis=("row", "col"))
 
 
 def shards(block_values, block_index, block_count, strength, raw_scores):

time: 918 us -> 1080 us (1.18)
  waiting for transfers between devices: 195 us -> 430 us
  blocking collectives: 616 us -> 541 us
    psum x5 -> x0, blocking collectives: 380 us -> none  [global_sum(): return lax.psum(partial_sum, ('row', 'col'))]
    unnamed x2 -> x6, blocking collectives: 120 us -> 427 us
    unnamed x6 -> x8, waiting for transfers between devices: 0.1 us -> 234 us
  transfers between devices with their start and end apart: 6 -> 7, of which waited for: 4 -> 5; matrix products, arithmetic and copies ran while one was open for 5% -> 4% of each run, Pallas kernels for 0% -> 0%
where the time goes in v1:
time: 1080 us
  blocking collectives  541 us (50%)
  waiting for transfers between devices  430 us (40%)
  matrix products  37.9 us (4%)
  other arithmetic  35.7 us (3%)
  local copies, waits for them, and re-layouts  20.2 us (2%)
  between operations  16.5 us (2%)
    unnamed x6, blocking collectives  427 us
    unnamed x8, waiting for transfers between devices  234 us
    reduce_scatter x3, waiting for transfers between devices, fold_terms(): lax.psum_scatter(row_part, 'col', scatter_dimension=0, tiled=True)  115 us
    reduce_scatter x3, waiting for transfers between devices, fold_terms(): lax.psum_scatter(col_part, 'row', scatter_dimension=0, tiled=True)  81.4 us
    all_gather x3, blocking collectives, shards(): panel_rows = lax.all_gather(direction, 'col', axis=0, tiled=True)  59.5 us
    all_gather x3, blocking collectives, shards(): panel_cols = lax.all_gather(direction, 'row', axis=0, tiled=True)  55.4 us
    dot_general x4, matrix products, local_terms(): jnp.einsum('crk,cik->cri', picked_cols, values, precision=lax.Precision.H...  22 us
  transfers between devices with their start and end apart: 7, of which 5 were waited for; matrix products, arithmetic and copies ran while one was open for 4% of the time, Pallas kernels for 0%

profile of v1, /device:TPU:1, one launch (start us, length us, event | category | flops | bytes accessed | tf_op | source)
XLA Modules:
  0.0 1082.4 jit_solution(5773921166962846330)
XLA Ops:
  7.2 0.8 compare_and_fusion
  8.0 0.8 slice_bitcast_fusion
  9.4 23.0 %all_gather.57 = f32[32,32,128]{2,1,0:T(8,128)S(1)} all-gather(f32[2,32,128]{2,1,0:T(8,128)} %param.13), channel_id=1, replica_groups=mesh['row'=16,'col'=16] {'col'}, dimensions={0}, use_global_device_ids=true | all-gather | bytes 557056 | tf_op jit(solution)/shard_map/all_gather | solution.py:61
  32.4 0.6 gather_fusion.3
  33.0 5.0 fusion.4
  38.1 4.9 scatter_fusion.1
  43.0 0.8 copy-done.3
  43.9 19.6 %all_gather.56 = f32[32,32,128]{2,1,0:T(8,128)S(1)} all-gather(f32[2,32,128]{2,1,0:T(8,128)S(1)} %copy-done.7), channel_id=1, replica_groups=mesh['row'=16,'col'=16] {'row'}, dimensions={0}, use_global_device_ids=true | all-gather | bytes 557056 | tf_op jit(solution)/shard_map/all_gather | solution.py:62
  63.4 1.4 gather_fusion.2
  64.9 6.2 fusion.5
  71.1 4.7 scatter_fusion
  75.8 0.8 copy-done.4
  76.7 0.6 gather_fusion
  77.3 0.6 gather_fusion.1
  77.9 0.6 dynamic-slice
  78.5 0.6 dynamic-slice.2
  80.5 4.3 fusion.7
  84.7 0.9 scatter_custom_fusion
  85.7 2.3 fusion.6
  88.0 0.7 scatter_custom_fusion.1
  88.7 58.4 %all-reduce.7 = f32[32,1,128]{2,0,1:T(8,128)S(1)} all-reduce(f32[32,1,128]{2,0,1:T(8,128)S(1)} %bitcast.49), channel_id=9, replica_groups=mesh['row'=16,'col'=16] {'row'}, use_global_device_ids=true, to_apply=%region_5.7.clone | all-reduce | flops 4096 | bytes 32768
  147.2 61.3 %all-reduce.6 = f32[32,1,128]{2,0,1:T(8,128)S(1)} all-reduce(f32[32,1,128]{2,0,1:T(8,128)S(1)} %bitcast.48), channel_id=8, replica_groups=mesh['row'=16,'col'=16] {'col'}, use_global_device_ids=true, to_apply=%region_3.5.clone | all-reduce | flops 4096 | bytes 32768
  208.5 1.0 multiply_reduce_fusion.4
  210.0 0.3 copy-done.8
  210.4 0.3 copy-done.9
  210.7 234.3 %all-reduce.11.cloned.1.call-done = (f32[8192]{0:T(1024)}, f32[8192]{0:T(1024)}) async-done(((f32[8192]{0:T(1024)}, f32[8192]{0:T(1024)}), (f32[8192]{0:T(1024)}, f32[8192]{0:T(1024)})) %all-reduce.11.cloned.1.call-update) | async-done | bytes 65552
  445.1 0.8 reshape.216
  445.9 0.8 reshape.217
  446.9 1.0 multiply_reduce_fusion.3
  447.9 0.3 dynamic-update-slice.2
  448.1 74.5 %all-reduce.2 = f32[8192]{0:T(1024)S(1)} all-reduce(f32[8192]{0:T(1024)S(1)} %dynamic-update-slice.2), channel_id=4, replica_groups=mesh['row'=16,'col'=16] {'row','col'}, use_global_device_ids=true, to_apply=%add.2 | all-reduce | flops 8192 | bytes 65536
  522.9 18.4 %all_gather.63 = f32[32,32,128]{2,1,0:T(8,128)S(1)} all-gather(f32[2,32,128]{2,1,0:T(8,128)S(1)} %multiply_add_fusion.4), channel_id=1, replica_groups=mesh['row'=16,'col'=16] {'col'}, dimensions={0}, use_global_device_ids=true | all-gather | bytes 557056 | tf_op jit(solution)/shard_map/all_gather | solution.py:61
  541.2 1.4 gather_fusion.5
  542.7 4.3 fusion.2
  547.1 4.7 scatter_fusion.3
  551.8 0.8 copy-done.5
  552.7 17.3 %all_gather.62 = f32[32,32,128]{2,1,0:T(8,128)S(1)} all-gather(f32[2,32,128]{2,1,0:T(8,128)S(1)} %multiply_add_fusion.4), channel_id=1, replica_groups=mesh['row'=16,'col'=16] {'row'}, dimensions={0}, use_global_device_ids=true | all-gather | bytes 557056 | tf_op jit(solution)/shard_map/all_gather | solution.py:62
  570.0 1.4 gather_fusion.4
  571.4 6.2 fusion.3
  577.6 4.7 scatter_fusion.2
  582.4 0.8 copy-done.6
  583.2 39.0 %reduce-scatter.15.cloned.1.call-done = f32[2,32,128]{2,1,0:T(8,128)} async-done(((f32[32,32,128]{2,1,0:T(8,128)}), f32[2,32,128]{2,1,0:T(8,128)}) %reduce-scatter.15.cloned.1.call-update) | async-done | bytes 32784 | tf_op jit(solution)/shard_map/reduce_scatter | solution.py:26
  622.3 57.2 %reduce-scatter.13.cloned.1.call-done = f32[2,32,128]{2,1,0:T(8,128)} async-done(((f32[32,32,128]{2,1,0:T(8,128)}), f32[2,32,128]{2,1,0:T(8,128)}) %reduce-scatter.13.cloned.1.call-update) | async-done | bytes 32784 | tf_op jit(solution)/shard_map/reduce_scatter | solution.py:26
  679.5 1.0 multiply_reduce_fusion.2
  680.4 0.3 dynamic-update-slice.3
  680.7 79.8 %all-reduce.3 = f32[8192]{0:T(1024)S(1)} all-reduce(f32[8192]{0:T(1024)S(1)} %dynamic-update-slice.3), channel_id=5, replica_groups=mesh['row'=16,'col'=16] {'row','col'}, use_global_device_ids=true, to_apply=%add.3 | all-reduce | flops 8192 | bytes 65536
  760.7 1.0 multiply_reduce_fusion.1
  761.6 0.3 dynamic-update-slice.4
  761.9 72.7 %all-reduce.4 = f32[8192]{0:T(1024)S(1)} all-reduce(f32[8192]{0:T(1024)S(1)} %dynamic-update-slice.4), channel_id=6, replica_groups=mesh['row'=16,'col'=16] {'row','col'}, use_global_device_ids=true, to_apply=%add.4 | all-reduce | flops 8192 | bytes 65536
  834.8 18.1 %all_gather.69 = f32[32,32,128]{2,1,0:T(8,128)S(1)} all-gather(f32[2,32,128]{2,1,0:T(8,128)S(1)} %multiply_add_fusion.2), channel_id=1, replica_groups=mesh['row'=16,'col'=16] {'col'}, dimensions={0}, use_global_device_ids=true | all-gather | bytes 557056 | tf_op jit(solution)/shard_map/all_gather | solution.py:61
  852.9 1.4 gather_fusion.7
  854.4 4.3 fusion
  858.8 4.7 scatter_fusion.5
  863.5 0.8 copy-done.1
  864.3 18.5 %all_gather.68 = f32[32,32,128]{2,1,0:T(8,128)S(1)} all-gather(f32[2,32,128]{2,1,0:T(8,128)S(1)} %multiply_add_fusion.2), channel_id=1, replica_groups=mesh['row'=16,'col'=16] {'row'}, dimensions={0}, use_global_device_ids=true | all-gather | bytes 557056 | tf_op jit(solution)/shard_map/all_gather | solution.py:62
  882.9 1.4 gather_fusion.6
  884.3 5.3 fusion.1
  889.7 2.7 scatter_fusion.4
  892.4 0.8 copy-done.2
  893.2 42.4 %reduce-scatter.19.cloned.1.call-done = f32[2,32,128]{2,1,0:T(8,128)} async-done(((f32[32,32,128]{2,1,0:T(8,128)}), f32[2,32,128]{2,1,0:T(8,128)}) %reduce-scatter.19.cloned.1.call-update) | async-done | bytes 32784 | tf_op jit(solution)/shard_map/reduce_scatter | solution.py:26
  935.5 57.4 %reduce-scatter.17.cloned.1.call-done = f32[2,32,128]{2,1,0:T(8,128)} async-done(((f32[32,32,128]{2,1,0:T(8,128)}), f32[2,32,128]{2,1,0:T(8,128)}) %reduce-scatter.17.cloned.1.call-update) | async-done | bytes 32784 | tf_op jit(solution)/shard_map/reduce_scatter | solution.py:26
  992.9 1.0 multiply_reduce_fusion
  994.1 79.8 %all-reduce.5 = f32[8192]{0:T(1024)S(1)} all-reduce(f32[8192]{0:T(1024)S(1)} %dynamic-update-slice.5), channel_id=7, replica_groups=mesh['row'=16,'col'=16] {'row','col'}, use_global_device_ids=true, to_apply=%add.5 | all-reduce | flops 8192 | bytes 65536
  1074.1 1.5 multiply_subtract_fusion
  (72 shorter events, 2.5 us)
Async XLA Ops:
  7.2 201.3 %reduce-scatter.11.cloned.1.call-start = ((), (), s32[]{:S(2)}) async-start(), calls=%async_computation.7 | async-start | bytes 557056 | tf_op jit(solution)/shard_map/reduce_scatter | solution.py:26
  33.0 10.9 %copy-start.7 = (f32[2,32,128]{2,1,0:T(8,128)S(1)}, f32[2,32,128]{2,1,0:T(8,128)}, u32[]{:S(2)}) copy-start(f32[2,32,128]{2,1,0:T(8,128)} %param.13) | copy-start | bytes 98308
  38.0 26.9 %copy-start = (f32[1,1,40,128,128]{4,3,2,1,0:T(8,128)S(1)}, f32[1,1,40,128,128]{4,3,2,1,0:T(8,128)}, u32[]{:S(2)}) copy-start(f32[1,1,40,128,128]{4,3,2,1,0:T(8,128)} %param.9) | copy-start | bytes 7864324
  42.9 0.8 copy-start.3
  43.8 164.7 %reduce-scatter.9.cloned.1.call-start = ((), (), s32[]{:S(2)}) async-start(), calls=%async_computation.6 | async-start | bytes 557056 | tf_op jit(solution)/shard_map/reduce_scatter | solution.py:26
  71.1 6.8 copy-start.12
  71.1 7.4 copy-start.11
  75.8 0.8 copy-start.4
  76.7 368.4 %all-reduce.11.cloned.1.call-start = ((), (), s32[]{:S(2)}) async-start(), calls=%async_computation.12 | async-start | bytes 131072
  80.5 128.1 %copy-start.10 = (f32[32]{0:T(128)S(1)}, f32[32]{0:T(128)}, u32[]{:S(2)}) copy-start(f32[32]{0:T(128)} %param.12) | copy-start | bytes 388
  209.8 0.6 copy-start.8
  210.0 0.6 copy-start.9
  210.7 411.6 %reduce-scatter.15.cloned.1.call-start = ((), (), s32[]{:S(2)}) async-start(), calls=%async_computation.9 | async-start | bytes 557056 | tf_op jit(solution)/shard_map/reduce_scatter | solution.py:26
  551.8 0.8 copy-start.5
  552.6 126.8 %reduce-scatter.13.cloned.1.call-start = ((), (), s32[]{:S(2)}) async-start(), calls=%async_computation.8 | async-start | bytes 557056 | tf_op jit(solution)/shard_map/reduce_scatter | solution.py:26
  582.4 0.8 copy-start.6
  583.2 352.4 %reduce-scatter.19.cloned.1.call-start = ((), (), s32[]{:S(2)}) async-start(), calls=%async_computation.11 | async-start | bytes 557056 | tf_op jit(solution)/shard_map/reduce_scatter | solution.py:26
  863.5 0.8 copy-start.1
  864.3 128.6 %reduce-scatter.17.cloned.1.call-start = ((), (), s32[]{:S(2)}) async-start(), calls=%async_computation.10 | async-start | bytes 557056 | tf_op jit(solution)/shard_map/reduce_scatter | solution.py:26
  892.3 0.8 copy-start.2
Sparse Core Ops, SparseCore 0:
  43.9 73.3 reduce-scatter.10
  120.0 55.2 reduce-scatter.8
  210.8 234.2 all-reduce.10
  552.7 69.4 reduce-scatter.14
  624.8 54.6 reduce-scatter.12
  864.4 71.0 reduce-scatter.18
  938.2 54.6 reduce-scatter.16
